TPU v7x, 32 devices: a whole 2x2x4 slice. The times are simulated.
32 devices in a mesh: groups: 2 (over y), strip: 4 (over z), angle: 2 (over x), depth: 2 (over core).
Axes of the slice: x: 2, y: 2, z: 4, core: 2. Of those that a mesh axis runs over, the one named last changes fastest.
Arguments:
- crystal: bfloat16 [16, 2, 512, 384], P(('groups', 'depth'), None, 'strip'), parts along dimension 0, may hold values from -4 to 4
- probe: bfloat16 [2, 256, 256], replicated, may hold values from -5 to 5
- amplitude: bfloat16 [4, 2048, 256], P('angle', ('groups', 'strip', 'depth')), parts along dimension 1, may hold values from 0.5 to 8
- shear: int32 [16, 8], P(('groups', 'angle'), 'depth'), parts along dimension 0, may hold values from 0 to 15
- scan_x: int32 [4, 4, 2], P(('groups', 'angle')), parts along dimension 0, may hold values from 0 to 112
- scan_y: int32 [4, 4, 2], P(('groups', 'angle')), parts along dimension 0, may hold values from 0 to 128
- slot_angle: int32 [4, 4, 2], P(('groups', 'angle')), parts along dimension 0, may hold values from 0 to 3
- owner_slot: int32 [4, 4, 2], P(('groups', 'angle')), parts along dimension 0, may hold values from 0 to 1, each once within a row
- counts: int32 [4, 4], P(('groups', 'angle')), parts along dimension 0, may hold values from 1 to 2
Outputs:
- gradient: float32 [16, 2, 512, 384], P(('groups', 'depth'), None, ('strip', 'angle')), parts along dimension 0
There are 2 independent parts, one for each index of `groups`. A program takes and returns all parts, laid end to end along the dimension named above; an argument that names none is the same for every part. Nothing has to cross between parts.
Inputs may be any that keep to these rules, and one draw needn't show every extreme that they name: `owner_slot`: for each angle group and home strip, the 2 entries are a permutation of 0 to 1.
All inputs are finite; a program needn't handle non-finite values.
Results may differ from a plain program's by a relative error of at most 0.02.
Values may be sent and summed in bfloat16 or wider, within the bound.
A program may use at most 64 MiB of HBM per device.

v0:
```python
import math

import jax
import jax.numpy as jnp
from jax import lax
from jax.sharding import PartitionSpec as P

FRAME = 256
WX = 128
SHEAR = 16
BAND = 144


def spot(*values):
    return tuple((jnp.asarray(value, jnp.int32) for value in values))


def dft_parts():
    index_row = jnp.arange(FRAME, dtype=jnp.int32)
    wound = index_row[:, None] * index_row[None, :] % FRAME
    phase = wound.astype(jnp.float32) * (2.0 * math.pi / FRAME)
    scaling = 1.0 / math.sqrt(FRAME)
    return (
        (jnp.cos(phase) * scaling).astype(jnp.bfloat16),
        (-jnp.sin(phase) * scaling).astype(jnp.bfloat16),
    )


def complex_times(left, right, sign):
    left_re = left[..., 0, :, :]
    left_im = left[..., 1, :, :]
    right_re = right[..., 0, :, :]
    right_im = right[..., 1, :, :]
    out_re = left_re * right_re - sign * left_im * right_im
    out_im = left_re * right_im + sign * left_im * right_re
    return jnp.stack([out_re, out_im], axis=-3)


def right_product(block, table_re, table_im, sign):
    part_re = block[..., 0, :, :]
    part_im = block[..., 1, :, :]

    def multiply(left, table):
        return jnp.einsum("...b,bc->...c", left, table, preferred_element_type=jnp.float32)

    first = multiply(part_re, table_re)
    second = multiply(part_im, table_im)
    third = multiply(part_re, table_im)
    fourth = multiply(part_im, table_re)
    return jnp.stack([first - sign * second, sign * third + fourth], axis=-3)


def body(crystal, probe, amplitude, shear, scan_x, scan_y, slot_angle, owner_slot, counts):
    strips = lax.axis_size("strip")
    strip_here = lax.axis_index("strip")
    layer_count = crystal.shape[0]
    slot_count = owner_slot.shape[2]
    quarter = strips // 4
    lanes = slot_count // quarter
    table_re, table_im = dft_parts()
    pad_re = jnp.pad(table_re, ((BAND, BAND), (0, 0)))
    pad_im = jnp.pad(table_im, ((BAND, BAND), (0, 0)))
    probe_pad = jnp.pad(probe, ((0, 0), (BAND, BAND), (0, 0)))
    offsets = scan_x[0]
    columns = scan_y[0]
    angles = slot_angle[0]
    owners = owner_slot[0]
    limits = counts[0]
    slot_ids = jnp.arange(slot_count, dtype=jnp.int32)
    reaches = jnp.arange(3, dtype=jnp.int32)
    home_rows = strip_here - reaches
    home_valid = (home_rows >= 0) & (home_rows <= strips - 3)
    home_safe = jnp.clip(home_rows, 0, strips - 1)
    sent_quota = owners[home_safe]
    sent_lane = sent_quota // quarter
    sent_alive = home_valid[:, None] & (slot_ids[None, :] < limits[home_safe][:, None])
    owner_strip = (home_safe[:, None] + 4 * (sent_quota % quarter) + 1) % strips
    destination = jnp.where(sent_alive, owner_strip * lanes + sent_lane, strips * lanes).reshape(-1)
    lift_rows = shear[angles[home_safe]].reshape(3 * slot_count, layer_count)
    corners = columns[home_safe].reshape(-1)
    crystal_pad = jnp.pad(crystal, ((0, 0), (0, 0), (SHEAR, SHEAR), (0, 0)))

    def project(lift_row, corner):
        gathered = jnp.zeros((2, BAND, FRAME), jnp.float32)
        for layer_index in range(layer_count):
            window = lax.dynamic_slice(
                crystal_pad[layer_index], spot(0, lift_row[layer_index], corner), (2, BAND, FRAME)
            )
            gathered = gathered + window.astype(jnp.float32)
        return gathered.astype(jnp.bfloat16)

    slab_bands = jax.vmap(project)(lift_rows, corners)
    outgoing = (
        jnp.zeros((strips * lanes, 2, BAND, FRAME), jnp.bfloat16)
        .at[destination]
        .set(slab_bands, mode="drop")
    )
    arrived = lax.all_to_all(outgoing, "strip", split_axis=0, concat_axis=0, tiled=True)
    quotas = jnp.arange(slot_count, dtype=jnp.int32)
    owned_lane = quotas // quarter
    source_home = (strip_here - 1 - 4 * (quotas % quarter)) % strips
    source_valid = source_home <= strips - 3
    matches = owners[source_home] == quotas[:, None]
    chosen = jnp.sum(jnp.where(matches, slot_ids[None, :], 0), axis=1)
    owned_alive = source_valid & (chosen < limits[source_home])
    owned_offset = offsets[source_home, chosen]
    row_starts = reaches[None, :] * WX - owned_offset[:, None] - SHEAR + BAND
    senders = (source_home[:, None] + reaches[None, :]) % strips
    sender_slots = senders * lanes + owned_lane[:, None]
    received = arrived[sender_slots]

    def take_rows(table, axis_pick):
        return jax.vmap(
            jax.vmap(lambda first_row: lax.dynamic_slice_in_dim(table, first_row, BAND, axis_pick))
        )(row_starts)

    rows_re = take_rows(pad_re, 0)
    rows_im = take_rows(pad_im, 0)
    probe_rows = take_rows(probe_pad, 1).astype(jnp.float32)
    exit_band = complex_times(probe_rows, received.astype(jnp.float32), 1.0).astype(jnp.bfloat16)
    section = right_product(exit_band, table_re, table_im, 1.0).astype(jnp.bfloat16)
    part_re = rows_re
    part_im = rows_im

    def multiply(table, block):
        return jnp.einsum("qkic,qkib->cqb", table, block, preferred_element_type=jnp.float32)

    spec_re = multiply(part_re, section[:, :, 0]) - multiply(part_im, section[:, :, 1])
    spec_im = multiply(part_im, section[:, :, 0]) + multiply(part_re, section[:, :, 1])
    spectrum = lax.psum_scatter(
        jnp.stack([spec_re, spec_im], axis=1).astype(jnp.bfloat16),
        "depth",
        scatter_dimension=0,
        tiled=True,
    ).astype(jnp.float32)
    spec_re = spectrum[:, 0]
    spec_im = spectrum[:, 1]
    magnitude = jnp.sqrt(spec_re * spec_re + spec_im * spec_im)
    measured = jnp.swapaxes(amplitude, 0, 1).astype(jnp.float32)
    factor = (1.0 - measured / jnp.maximum(magnitude, 1.0)) * owned_alive[None, :, None].astype(
        jnp.float32
    )
    residual = (spectrum * factor[:, None]).astype(jnp.bfloat16)
    inverse_rows = right_product(residual, table_re, table_im, -1.0).astype(jnp.bfloat16)
    half_rows = inverse_rows.shape[0]
    column_start = lax.axis_index("depth") * half_rows
    home_owned = jnp.where(owned_alive[:, None], sender_slots, strips * lanes).reshape(-1)
    share_rows = BAND // lax.axis_size("depth")
    first_row = jnp.int32(0)
    part_re = lax.dynamic_slice(
        rows_re,
        spot(0, 0, first_row, column_start),
        (slot_count, 3, lax.axis_size("depth") * share_rows, half_rows),
    )
    part_im = lax.dynamic_slice(
        rows_im,
        spot(0, 0, first_row, column_start),
        (slot_count, 3, lax.axis_size("depth") * share_rows, half_rows),
    )

    def multiply(table, block):
        return jnp.einsum("qkic,cqb->qkib", table, block, preferred_element_type=jnp.float32)

    wave_re = multiply(part_re, inverse_rows[:, 0]) + multiply(part_im, inverse_rows[:, 1])
    wave_im = multiply(part_re, inverse_rows[:, 1]) - multiply(part_im, inverse_rows[:, 0])
    pieces = lax.psum_scatter(
        jnp.moveaxis(
            complex_times(probe_rows, jnp.stack([wave_re, wave_im], axis=2), -1.0), 3, 0
        ).astype(jnp.bfloat16),
        "depth",
        scatter_dimension=0,
        tiled=True,
    ).astype(jnp.float32)
    pieces = (
        jnp.moveaxis(pieces, 0, 3)
        .astype(jnp.bfloat16)
        .reshape(slot_count * 3, 2, share_rows, FRAME)
    )
    returning = (
        jnp.zeros((strips * lanes, 2, share_rows, FRAME), jnp.bfloat16)
        .at[home_owned]
        .set(pieces, mode="drop")
    )
    returned = lax.all_to_all(returning, "strip", split_axis=0, concat_axis=0, tiled=True)
    returned = lax.all_gather(returned, "depth", axis=2, tiled=True)
    back_bands = returned[(owner_strip * lanes + sent_lane).reshape(-1)]
    weights = sent_alive.reshape(-1).astype(jnp.float32)

    def deposit(item_index, gradient_pad):
        contribution = back_bands[item_index].astype(jnp.float32) * weights[item_index]
        lift_row = lift_rows[item_index]
        corner = corners[item_index]
        for layer_index in range(layer_count):
            position = spot(layer_index, 0, lift_row[layer_index], corner)
            current = lax.dynamic_slice(gradient_pad, position, (1, 2, BAND, FRAME))
            gradient_pad = lax.dynamic_update_slice(
                gradient_pad, current + contribution[None], position
            )
        return gradient_pad

    start_pad = jnp.zeros((layer_count, 2, WX + 2 * SHEAR, crystal.shape[3]), jnp.float32)
    gradient_pad = lax.fori_loop(0, 3 * slot_count, deposit, start_pad)
    gradient = gradient_pad[:, :, SHEAR : SHEAR + WX].astype(jnp.bfloat16)
    angle_count = lax.axis_size("angle")
    scaling = 1.0 / (shear.shape[0] * angle_count)
    shared = lax.psum_scatter(gradient, "angle", scatter_dimension=2, tiled=True).astype(
        jnp.float32
    )
    return shared * scaling


def solution(mesh):
    placed = (
        P(("groups", "depth"), None, "strip", None),
        P(),
        P("angle", ("groups", "strip", "depth"), None),
        P(("groups", "angle"), "depth"),
        P(("groups", "angle"), None, None),
        P(("groups", "angle"), None, None),
        P(("groups", "angle"), None, None),
        P(("groups", "angle"), None, None),
        P(("groups", "angle"), None),
    )
    return jax.shard_map(
        body,
        mesh=mesh,
        in_specs=placed,
        out_specs=P(("groups", "depth"), None, ("strip", "angle"), None),
        check_vma=False,
    )
```

profile of v0, /device:TPU:0, one launch (start us, length us, event | category | flops | bytes accessed | tf_op | source)
XLA Modules:
  0.0 371.9 jit_solution(13340963413556306195)
XLA Ops:
  11.7 12.6 %while.21 = (s32[]{:T(128)}, bf16[2,160,384]{2,1,0:T(8,128)(2,1)S(1)}, s32[6,3]{1,0:T(8,128)S(1)}, bf16[6,2,144,256]{3,2,1,0:T(8,128)(2,1)S(1)}, s32[]{:T(128)}) while((s32[]{:T(128)}, bf16[2,160,384]{2,1,0:T(8,128)(2,1)S(1)}, s32[6,3]{1,0:T(8,128)S(1)}, bf16[6,2,144,256]{3,2,1,0:T(8,128)(2,1)S(1)}, s32[]{:T(128)}) %tuple.156), condition=%wide.while_cond.1, body=%wide.while_body.1.sunk | while | flops 2 | bytes 295029 | solution.py:86
  24.4 12.9 %while.22 = (s32[]{:T(128)}, bf16[2,160,384]{2,1,0:T(8,128)(2,1)S(1)}, s32[6,3]{1,0:T(8,128)S(1)}, bf16[6,2,144,256]{3,2,1,0:T(8,128)(2,1)S(1)}, s32[]{:T(128)}) while((s32[]{:T(128)}, bf16[2,160,384]{2,1,0:T(8,128)(2,1)S(1)}, s32[6,3]{1,0:T(8,128)S(1)}, bf16[6,2,144,256]{3,2,1,0:T(8,128)(2,1)S(1)}, s32[]{:T(128)}) %tuple.153), condition=%wide.while_cond.2, body=%wide.while_body.2.sunk | while | flops 2 | bytes 295029 | solution.py:86
  37.3 12.4 %while.23 = (s32[]{:T(128)}, bf16[2,160,384]{2,1,0:T(8,128)(2,1)S(1)}, s32[6,3]{1,0:T(8,128)S(1)}, bf16[6,2,144,256]{3,2,1,0:T(8,128)(2,1)S(1)}, s32[]{:T(128)}) while((s32[]{:T(128)}, bf16[2,160,384]{2,1,0:T(8,128)(2,1)S(1)}, s32[6,3]{1,0:T(8,128)S(1)}, bf16[6,2,144,256]{3,2,1,0:T(8,128)(2,1)S(1)}, s32[]{:T(128)}) %tuple.150), condition=%wide.while_cond.3, body=%wide.while_body.3.sunk | while | flops 2 | bytes 295029 | solution.py:86
  50.8 15.6 %while.24 = (s32[]{:T(128)}, bf16[2,160,384]{2,1,0:T(8,128)(2,1)S(1)}, s32[6,3]{1,0:T(8,128)S(1)}, bf16[6,2,144,256]{3,2,1,0:T(8,128)(2,1)}, s32[]{:T(128)}) while((s32[]{:T(128)}, bf16[2,160,384]{2,1,0:T(8,128)(2,1)S(1)}, s32[6,3]{1,0:T(8,128)S(1)}, bf16[6,2,144,256]{3,2,1,0:T(8,128)(2,1)}, s32[]{:T(128)}) %tuple.147), condition=%wide.while_cond.4, body=%wide.while_body.4.sunk | while | flops 2 | bytes 296553 | solution.py:86
  75.3 6.5 %all-to-all-start = ((bf16[8,2,144,256]{3,2,1,0:T(8,128)(2,1)}), bf16[8,2,144,256]{3,2,1,0:T(8,128)(2,1)}, u32[]{:S(2)}, u32[]{:S(2)}) async-start(bf16[8,2,144,256]{3,2,1,0:T(8,128)(2,1)} %scatter_fusion), calls=%async_computation | async-start | bytes 2359296 | tf_op jit(solution)/shard_map/all_to_all | solution.py:98
  85.0 7.5 %while.25 = (s32[]{:T(128)}, bf16[544,256]{1,0:T(8,128)(2,1)S(1)}, s32[6,2]{0,1:T(2,128)S(1)}, bf16[6,144,256]{2,1,0:T(8,128)(2,1)S(1)}, s32[]{:T(128)}) while((s32[]{:T(128)}, bf16[544,256]{1,0:T(8,128)(2,1)S(1)}, s32[6,2]{0,1:T(2,128)S(1)}, bf16[6,144,256]{2,1,0:T(8,128)(2,1)S(1)}, s32[]{:T(128)}) %tuple.162), condition=%wide.while_cond.5, body=%wide.while_body.5.sunk | while | flops 2 | bytes 147553 | solution.py:114
  98.0 7.3 %while.20 = (s32[]{:T(128)}, bf16[544,256]{1,0:T(8,128)(2,1)S(1)}, s32[6,2]{0,1:T(2,128)S(1)}, bf16[6,144,256]{2,1,0:T(8,128)(2,1)S(1)}, s32[]{:T(128)}) while((s32[]{:T(128)}, bf16[544,256]{1,0:T(8,128)(2,1)S(1)}, s32[6,2]{0,1:T(2,128)S(1)}, bf16[6,144,256]{2,1,0:T(8,128)(2,1)S(1)}, s32[]{:T(128)}) %tuple.176), condition=%wide.while_cond, body=%wide.while_body.sunk | while | flops 2 | bytes 147553 | solution.py:114
  105.3 5.2 %all-to-all-done = bf16[8,2,144,256]{3,2,1,0:T(8,128)(2,1)} async-done(((bf16[8,2,144,256]{3,2,1,0:T(8,128)(2,1)}), bf16[8,2,144,256]{3,2,1,0:T(8,128)(2,1)}, u32[]{:S(2)}, u32[]{:S(2)}) %all-to-all-start) | async-done | bytes 1179680 | tf_op jit(solution)/shard_map/all_to_all | solution.py:98
  121.5 6.1 %reduce-scatter.10.cloned.1.call-done = bf16[128,1024]{1,0:T(8,128)(2,1)} async-done(((bf16[256,1024]{1,0:T(8,128)(2,1)}), bf16[128,1024]{1,0:T(8,128)(2,1)}) %reduce-scatter.10.cloned.1.call-update) | async-done | bytes 262160
  138.3 9.0 %reduce-scatter.12.cloned.1.call-done = bf16[72,3072]{1,0:T(8,128)(2,1)} async-done(((bf16[144,3072]{1,0:T(8,128)(2,1)}), bf16[72,3072]{1,0:T(8,128)(2,1)}) %reduce-scatter.12.cloned.1.call-update) | async-done | bytes 442384
  150.3 21.1 %all_to_all.10 = bf16[8,2,72,256]{3,2,1,0:T(8,128)(2,1)} all-to-all(bf16[8,2,72,256]{3,2,1,0:T(8,128)(2,1)S(1)} %scatter_fusion.1), channel_id=1, replica_groups=mesh['groups'=2,'strip'=4,'angle'=2,'depth'=2] {'strip'}, dimensions={0} | all-to-all | bytes 1179648 | tf_op jit(solution)/shard_map/all_to_all | solution.py:184
  172.0 7.9 %all-gather.2.cloned.1.call-done = bf16[8,2,144,256]{3,2,1,0:T(8,128)(2,1)} async-done(((bf16[8,2,72,256]{3,2,1,0:T(8,128)(2,1)}), bf16[8,2,144,256]{3,2,1,0:T(8,128)(2,1)}) %all-gather.2.cloned.1.call-update) | async-done | bytes 1179664 | tf_op jit(solution)/shard_map/all_gather | solution.py:185
  181.9 162.8 %while.19 = (s32[]{:T(128)}, f32[4,2,160,384]{3,2,1,0:T(8,128)S(1)}, s32[6,4]{1,0:T(8,128)S(1)}, s32[6]{0:T(128)S(1)}, bf16[6,2,144,256]{3,2,1,0:T(8,128)(2,1)S(...) while((s32[]{:T(128)}, ...), condition=%wide.region_6.7_spmd, body=%wide.region_5.6_spmd.sunk | while | flops 884753 | bytes 5308875 | solution.py:202
  188.9 3.0 dynamic_update_slice.32
  194.7 3.0 dynamic_update_slice.33
  200.4 3.0 dynamic_update_slice.34
  206.1 3.0 dynamic_update_slice.35
  216.1 3.0 dynamic_update_slice.32
  221.8 3.0 dynamic_update_slice.33
  233.2 3.0 dynamic_update_slice.35
  243.2 3.0 dynamic_update_slice.32
  248.9 3.0 dynamic_update_slice.33
  254.6 3.0 dynamic_update_slice.34
  260.4 3.0 dynamic_update_slice.35
  276.0 3.0 dynamic_update_slice.33
  287.4 3.0 dynamic_update_slice.35
  297.4 3.0 dynamic_update_slice.32
  303.2 3.0 dynamic_update_slice.33
  308.9 3.0 dynamic_update_slice.34
  330.3 3.0 dynamic_update_slice.33
  341.7 3.0 dynamic_update_slice.35
  345.7 17.7 %reduce-scatter.8.cloned.1.call-done = bf16[4,2,64,384]{3,2,1,0:T(8,128)(2,1)} async-done(((bf16[4,2,128,384]{3,2,1,0:T(8,128)(2,1)}), bf16[4,2,64,384]{3,2,1,0:T(8,128)(2,1)}) %reduce-scatter.8.cloned.1.call-update) | async-done | bytes 393232 | tf_op jit(solution)/shard_map/reduce_scatter | solution.py:206
  (303 shorter events, 170.8 us)
Async XLA Ops:
  6.5 4.4 %copy-start = (s32[4,4]{1,0:T(4,128)S(1)}, s32[4,4]{1,0:T(4,128)}, u32[]{:S(2)}) copy-start(s32[4,4]{1,0:T(4,128)} %param.14) | copy-start | bytes 196
  37.3 29.1 %copy-start.1 = (s32[1,4]{1,0:T(1,128)S(1)}, s32[1,4]{1,0:T(1,128)}, u32[]{:S(2)}) copy-start(s32[1,4]{1,0:T(1,128)} %param.19) | copy-start | bytes 52
  49.7 19.6 %copy-start.3 = (bf16[6,2,144,256]{3,2,1,0:T(8,128)(2,1)}, bf16[6,2,144,256]{3,2,1,0:T(8,128)(2,1)S(1)}, u32[]{:S(2)}) copy-start(bf16[6,2,144,256]{3,2,1,0:T(8,128)(2,1)S(1)} %get-tuple-element.146) | copy-start | bytes 2654212
  49.7 18.1 %copy-start.9 = (s32[1,4,2]{1,2,0:T(2,128)S(1)}, s32[1,4,2]{1,2,0:T(2,128)}, u32[]{:S(2)}) copy-start(s32[1,4,2]{1,2,0:T(2,128)} %param.18) | copy-start | bytes 100
  75.3 8.9 %copy-start.2 = (s32[1,4,2]{1,2,0:T(2,128)S(1)}, s32[1,4,2]{1,2,0:T(2,128)}, u32[]{:S(2)}) copy-start(s32[1,4,2]{1,2,0:T(2,128)} %param.15) | copy-start | bytes 100
  75.3 35.2 %all-to-all-start = ((bf16[8,2,144,256]{3,2,1,0:T(8,128)(2,1)}), bf16[8,2,144,256]{3,2,1,0:T(8,128)(2,1)}, u32[]{:S(2)}, u32[]{:S(2)}) async-start(bf16[8,2,144,256]{3,2,1,0:T(8,128)(2,1)} %scatter_fusion), calls=%async_computation | async-start | bytes 2359296 | tf_op jit(solution)/shard_map/all_to_all | solution.py:98
  81.8 10.9 %copy-start.4 = (bf16[2,256,256]{2,1,0:T(8,128)(2,1)S(1)}, bf16[2,256,256]{2,1,0:T(8,128)(2,1)}, u32[]{:S(2)}) copy-start(bf16[2,256,256]{2,1,0:T(8,128)(2,1)} %param.12) | copy-start | bytes 786436
  81.8 45.8 %reduce-scatter.10.cloned.1.call-start = ((), (), s32[]{:S(2)}) async-start(), calls=%async_computation.7 | async-start | bytes 786432
  82.9 10.5 %copy-start.7 = (s32[1024]{0:T(1024)}, s32[1024]{0:T(1024)S(1)}, u32[]{:S(2)}) copy-start(s32[1024]{0:T(1024)S(1)} %pad_clamp_fusion.2) | copy-start | bytes 12292
  83.6 0.6 copy-start.10
  119.4 2.1 copy-start.11
  119.4 9.5 %copy-start.5 = (bf16[2,128,256]{2,1,0:T(8,128)(2,1)S(1)}, bf16[2,128,256]{2,1,0:T(8,128)(2,1)}, u32[]{:S(2)}) copy-start(bf16[2,128,256]{2,1,0:T(8,128)(2,1)} %param.13) | copy-start | bytes 393220
  120.5 26.9 %reduce-scatter.12.cloned.1.call-start = ((), (), s32[]{:S(2)}) async-start(), calls=%async_computation.8 | async-start | bytes 1327104
  137.8 42.1 %all-gather.2.cloned.1.call-start = ((), (), s32[]{:S(2)}) async-start(), calls=%async_computation.5 | async-start | bytes 1769472 | tf_op jit(solution)/shard_map/all_gather | solution.py:185
  149.3 22.6 %copy-start.6 = (f32[3,2]{1,0:T(4,128)S(1)}, f32[3,2]{1,0:T(4,128)}, u32[]{:S(2)}) copy-start(f32[3,2]{1,0:T(4,128)} %get-tuple-element.313) | copy-start | bytes 76
  149.3 22.7 %copy-start.8 = (s32[6]{0:T(128)S(1)}, s32[6]{0:T(128)}, u32[]{:S(2)}) copy-start(s32[6]{0:T(128)} %get-tuple-element.251) | copy-start | bytes 76
  171.5 191.9 %reduce-scatter.8.cloned.1.call-start = ((), (), s32[]{:S(2)}) async-start(), calls=%async_computation.6 | async-start | bytes 1179648 | tf_op jit(solution)/shard_map/reduce_scatter | solution.py:206
Sparse Core Ops, SparseCore 0:
  120.6 6.9 reduce-scatter.9
  138.0 9.3 reduce-scatter.11
  171.6 8.2 all-gather.1
  345.8 17.5 reduce-scatter.7
where the time goes:
time: 374 us; the launch traced here: 372 us
  local copies, waits for them, and re-layouts  182 us (49%)
  loops' own time  60.1 us (16%)
  waiting for transfers between devices  46 us (12%)
  other arithmetic  29.5 us (8%)
  blocking collectives  21.1 us (6%)
  between operations  13.6 us (4%)
  matrix products  12.1 us (3%)
  starting transfers between devices  7.15 us (2%)
    dynamic_update_slice x24, local copies, waits for them, and re-layouts, deposit(): lax.dynamic_update_slice(gradient_pad, current + contribution[None], posi...  71.4 us
    gather x108, local copies, waits for them, and re-layouts  67.2 us
    another operation x1, loops' own time, body(): gradient_pad = lax.fori_loop(0, 3 * slot_count, deposit, start_pad)  59.2 us
    all_to_all x1, blocking collectives, body(): lax.all_to_all(returning, 'strip', split_axis=0, concat_axis=0, tiled=True)  21.1 us
    add x24, other arithmetic, deposit(): current + contribution[None]  20.2 us
    reduce_scatter x1, waiting for transfers between devices, body(): lax.psum_scatter(gradient, 'angle', scatter_dimension=2, tiled=True)  17.7 us
    unnamed x6, waiting for transfers between devices  15.2 us
    dot_general x8, matrix products, multiply(): jnp.einsum('...b,bc->...c', left, table, preferred_element_type=jnp.float32)  9.44 us
  transfers between devices with their start and end apart: 5, of which 5 were waited for; matrix products, arithmetic and copies ran while one was open for 6% of the time, Pallas kernels for 0%

commit v1 on v0

v1 whole, which is shorter than its diff:
```python
import functools

import jax
import jax.numpy as jnp
import numpy as np
from jax import lax
from jax.experimental import pallas as pl
from jax.experimental.pallas import tpu as pltpu
from jax.sharding import PartitionSpec as P

FRAME = 256
WX = 128
REACHES = 3
ROWS = (WX, FRAME, FRAME - WX)
BASES = (0, 0, WX)
MESH = pl.DeviceIdType.MESH


def dft_tables():
    index_row = np.arange(FRAME)
    phase = (index_row[:, None] * index_row[None, :] % FRAME) * (2.0 * np.pi / FRAME)
    real = np.cos(phase) / np.sqrt(FRAME)
    imag = -np.sin(phase) / np.sqrt(FRAME)
    table = np.block([[real, imag], [-imag, real]]).astype(np.float32)
    return jnp.asarray(table, jnp.bfloat16), jnp.asarray(table.T, jnp.bfloat16)


def dot(left, right):
    return jnp.dot(left, right, preferred_element_type=jnp.float32)


def differences(rows, columns):
    shape = (rows, columns)
    return lax.broadcasted_iota(jnp.int32, shape, 1) - lax.broadcasted_iota(jnp.int32, shape, 0)


def one_hot(mask):
    return jnp.where(mask, 1.0, 0.0).astype(jnp.bfloat16)


def kernel(
    sizes,
    crystal,
    probe,
    amplitude,
    table,
    table_t,
    shear,
    scan_x,
    scan_y,
    slot_angle,
    owner_slot,
    counts,
    out,
    film,
    sent0,
    sent1,
    sent2,
    got0,
    got1,
    got2,
    measured,
    back,
    home0,
    home1,
    home2,
    placed,
    total,
    grad_out,
    grad_in,
    film_send,
    film_recv,
    amp_send,
    amp_recv,
    back_send,
    back_recv,
    grad_send,
    grad_recv,
):
    strips, angle_devs, depths, layers, slots, columns = sizes
    quarter = strips // 4
    half = slots // depths
    share = WX // angle_devs
    sent = (sent0, sent1, sent2)
    got = (got0, got1, got2)
    homes = (home0, home1, home2)
    s = lax.axis_index("strip")
    a = lax.axis_index("angle")
    d = lax.axis_index("depth")

    def rcopy(source, target, send_sem, recv_sem, **where):
        return pltpu.make_async_remote_copy(
            source, target, send_sem, recv_sem, device_id=where, device_id_type=MESH
        )

    def wrap(strip):
        return lax.rem(strip + 4 * strips, strips)

    barrier = pltpu.get_barrier_semaphore()
    shifts = set()
    for k in range(REACHES):
        for t in range(quarter):
            shifts |= {(1 - k + 4 * t) % strips, (k - 1 - 4 * t) % strips}
    expected = jnp.int32(angle_devs - 1 + depths - 1)
    for step in range(1, angle_devs):
        pl.semaphore_signal(
            barrier, 1, device_id={"angle": lax.rem(a + step, angle_devs)}, device_id_type=MESH
        )
    for step in range(1, depths):
        pl.semaphore_signal(
            barrier, 1, device_id={"depth": lax.rem(d + step, depths)}, device_id_type=MESH
        )
    for shift in sorted(shifts - {0}):
        peer = wrap(s + shift)
        if quarter == 1:
            close = jnp.abs(peer - s) == 1
        else:
            close = peer >= 0
        expected = expected + jnp.where(close, depths, 0)

        @pl.when(close)
        def _():
            for other in range(depths):
                pl.semaphore_signal(
                    barrier, 1, device_id={"strip": peer, "depth": other}, device_id_type=MESH
                )

    for layer in range(layers):
        for part in range(2):
            film[layer * WX : (layer + 1) * WX, part * columns : (part + 1) * columns] = crystal[
                layer, part
            ]
    pl.semaphore_wait(barrier, expected)

    def pick(ref, home, quota):
        value = jnp.int32(0)
        for m in range(slots):
            value = value + jnp.where(owner_slot[0, home, m] == quota, ref[0, home, m], 0)
        return value

    for other in range(depths):
        block = amplitude.at[other * half : (other + 1) * half]

        @pl.when(d != other)
        def _():
            rcopy(block, measured.at[d], amp_send.at[other], amp_recv.at[d], depth=other).start()

        @pl.when(d == other)
        def _():
            measured[d] = amplitude[other * half : (other + 1) * half]

    def film_copy(k, q):
        owner = wrap(s - k + 4 * (q % quarter) + 1)
        return rcopy(
            sent[k].at[q],
            got[k].at[d, q % half],
            film_send.at[k, q],
            film_recv.at[k, d, q % half],
            strip=owner,
            depth=q // half,
        )

    def own_strip(k, q):
        return (1 - k + 4 * (q % quarter)) % strips == 0

    for k in (0, 2, 1):
        home = s - k
        rows = ROWS[k]

        @pl.when((home >= 0) & (home <= strips - 3))
        def _():
            for q in range(slots):
                offset = pick(scan_x, home, q) - WX * k + BASES[k]
                angle = pick(slot_angle, home, q)
                corner = pick(scan_y, home, q)
                gap = differences(rows, WX)
                picks = jnp.concatenate(
                    [one_hot(gap == offset + shear[angle, z]) for z in range(layers)], axis=1
                )
                tall = dot(picks, film[...]).astype(jnp.bfloat16)
                window = one_hot(differences(FRAME, columns) == corner).T
                wave = jnp.concatenate(
                    [dot(tall[:, :columns], window), dot(tall[:, columns:], window)], axis=1
                ).astype(jnp.bfloat16)
                if own_strip(k, q):

                    @pl.when(d == q // half)
                    def _():
                        got[k][d, q % half] = wave

                    @pl.when(d != q // half)
                    def _():
                        sent[k][q] = wave
                        film_copy(k, q).start()
                else:
                    sent[k][q] = wave
                    film_copy(k, q).start()

    for other in range(depths):

        @pl.when(d != other)
        def _():
            rcopy(
                amplitude.at[other * half : (other + 1) * half],
                measured.at[other],
                amp_send.at[other],
                amp_recv.at[other],
                depth=other,
            ).wait_recv()

    for lane in range(half):
        quota = d * half + lane
        home = wrap(s - 1 - 4 * lax.rem(quota, quarter))

        @pl.when(home <= strips - 3)
        def _():
            for k in (1, 0, 2):
                for source in range(depths):
                    local = (wrap(home + k) == s) & (d == source)

                    @pl.when(jnp.logical_not(local))
                    def _():
                        rcopy(
                            sent[k].at[lane],
                            got[k].at[source, lane],
                            film_send.at[k, lane],
                            film_recv.at[k, source, lane],
                            strip=wrap(home + k),
                            depth=source,
                        ).wait_recv()

            def gathered(ref, low, high):
                value = ref[0, lane, low:high].astype(jnp.float32)
                for source in range(1, depths):
                    value = value + ref[source, lane, low:high].astype(jnp.float32)
                return value

            whole = jnp.concatenate(
                [
                    gathered(got1, 0, WX) + gathered(got0, 0, WX),
                    gathered(got1, WX, FRAME) + gathered(got2, 0, FRAME - WX),
                ],
                axis=0,
            )
            probe_re = probe[0].astype(jnp.float32)
            probe_im = probe[1].astype(jnp.float32)
            film_re, film_im = whole[:, :FRAME], whole[:, FRAME:]
            exit_wave = jnp.concatenate(
                [probe_re * film_re - probe_im * film_im, probe_re * film_im + probe_im * film_re],
                axis=1,
            ).astype(jnp.bfloat16)
            section = dot(exit_wave, table[...]).astype(jnp.bfloat16)
            spectrum = dot(
                table_t[...], jnp.concatenate([section[:, :FRAME], section[:, FRAME:]], axis=0)
            )
            spec_re, spec_im = spectrum[:FRAME], spectrum[FRAME:]
            magnitude = jnp.sqrt(spec_re * spec_re + spec_im * spec_im)
            levels = jnp.concatenate(
                [measured[source, lane] for source in range(depths)], axis=0
            ).astype(jnp.float32)
            slot = jnp.int32(0)
            for m in range(slots):
                slot = slot + jnp.where(owner_slot[0, home, m] == quota, m, 0)
            live = jnp.where(slot < counts[0, home], 1.0, 0.0).astype(jnp.float32)
            factor = (1.0 - levels / jnp.maximum(magnitude, 1.0)) * live
            residual = jnp.concatenate([spec_re * factor, spec_im * factor], axis=1).astype(
                jnp.bfloat16
            )
            inverse = dot(residual, table_t[...]).astype(jnp.bfloat16)
            wave = dot(
                table[...], jnp.concatenate([inverse[:, :FRAME], inverse[:, FRAME:]], axis=0)
            )
            wave_re, wave_im = wave[:FRAME], wave[FRAME:]
            back[lane] = jnp.concatenate(
                [probe_re * wave_re + probe_im * wave_im, probe_re * wave_im - probe_im * wave_re],
                axis=1,
            ).astype(jnp.bfloat16)

    def back_copy(k, q, home, other):
        return rcopy(
            back.at[q % half, BASES[k] : BASES[k] + ROWS[k]],
            homes[k].at[q],
            back_send.at[k, q % half, other],
            back_recv.at[k, q],
            strip=wrap(home + k),
            depth=other,
        )

    def returns(act, keep):
        for q in range(slots):
            home = wrap(s - 1 - 4 * (q % quarter))

            @pl.when((home <= strips - 3) & (d == q // half))
            def _():
                for k in (0, 2, 1):
                    for other in range(depths):
                        if own_strip(k, q) and other == q // half:
                            if keep:
                                homes[k][q] = back[q % half, BASES[k] : BASES[k] + ROWS[k]]
                        else:
                            act(back_copy(k, q, home, other))

    returns(lambda copy: copy.start(), True)

    for k in range(REACHES):
        home = s - k
        rows = ROWS[k]
        base = sum(ROWS[:k]) * slots

        @pl.when((home >= 0) & (home <= strips - 3))
        def _():
            for q in range(slots):
                if own_strip(k, q):

                    @pl.when(d != q // half)
                    def _():
                        back_copy(k, q, home, q // half).wait_recv()
                else:
                    back_copy(k, q, home, q // half).wait_recv()
                corner = pick(scan_y, home, q)
                window = one_hot(differences(FRAME, columns) == corner)
                value = homes[k][q]
                placed[base + q * rows : base + (q + 1) * rows, :columns] = dot(
                    value[:, :FRAME], window
                ).astype(jnp.bfloat16)
                placed[base + q * rows : base + (q + 1) * rows, columns:] = dot(
                    value[:, FRAME:], window
                ).astype(jnp.bfloat16)

    def grad_copy(step, z):
        other = lax.rem(a + step, angle_devs)
        return rcopy(
            grad_out.at[other, z],
            grad_in.at[step, z],
            grad_send.at[step, z],
            grad_recv.at[step, z],
            angle=other,
        )

    for z in range(layers):
        total[...] = jnp.zeros_like(total)
        for k in range(REACHES):
            home = s - k
            rows = ROWS[k]
            base = sum(ROWS[:k]) * slots

            @pl.when((home >= 0) & (home <= strips - 3))
            def _():
                picks = []
                for q in range(slots):
                    offset = pick(scan_x, home, q) - WX * k + BASES[k]
                    lift = shear[pick(slot_angle, home, q), z]
                    picks.append(one_hot(differences(WX, rows) == -(offset + lift)))
                total[...] += dot(
                    jnp.concatenate(picks, axis=1), placed[base : base + slots * rows]
                )

        for other in range(angle_devs):
            grad_out[other, z] = total[other * share : (other + 1) * share].astype(jnp.bfloat16)
        for step in range(1, angle_devs):
            grad_copy(step, z).start()

    scaling = 1.0 / (shear.shape[0] * angle_devs)
    for z in range(layers):
        value = grad_out[a, z].astype(jnp.float32)
        for step in range(1, angle_devs):
            grad_copy(step, z).wait_recv()
            value = value + grad_in[step, z].astype(jnp.float32)
        value = value * scaling
        for part in range(2):
            out[z, part] = value[:, part * columns : (part + 1) * columns]

    for other in range(depths):

        @pl.when(d != other)
        def _():
            rcopy(
                amplitude.at[other * half : (other + 1) * half],
                measured.at[d],
                amp_send.at[other],
                amp_recv.at[d],
                depth=other,
            ).wait_send()

    for k in range(REACHES):
        home = s - k

        @pl.when((home >= 0) & (home <= strips - 3))
        def _():
            for q in range(slots):
                if own_strip(k, q):

                    @pl.when(d != q // half)
                    def _():
                        film_copy(k, q).wait_send()
                else:
                    film_copy(k, q).wait_send()

    returns(lambda copy: copy.wait_send(), False)
    for z in range(layers):
        for step in range(1, angle_devs):
            grad_copy(step, z).wait_send()


def body(sizes_of, crystal, probe, amplitude, shear, scan_x, scan_y, slot_angle, owner_slot, counts):
    strips, angle_devs, depths = sizes_of
    layers, _, _, columns = crystal.shape
    slots = owner_slot.shape[2]
    half = slots // depths
    share = WX // angle_devs
    table, table_t = dft_tables()
    bf16 = jnp.bfloat16
    vmem = pl.BlockSpec(memory_space=pltpu.VMEM)
    smem = pl.BlockSpec(memory_space=pltpu.SMEM)
    dma = pltpu.SemaphoreType.DMA
    scratch = [pltpu.VMEM((layers * WX, 2 * columns), bf16)]
    scratch += [pltpu.VMEM((slots, rows, 2 * FRAME), bf16) for rows in ROWS]
    scratch += [pltpu.VMEM((depths, half, rows, 2 * FRAME), bf16) for rows in ROWS]
    scratch += [
        pltpu.VMEM((depths, half, FRAME // depths, FRAME), bf16),
        pltpu.VMEM((half, FRAME, 2 * FRAME), bf16),
    ]
    scratch += [pltpu.VMEM((slots, rows, 2 * FRAME), bf16) for rows in ROWS]
    scratch += [
        pltpu.VMEM((sum(ROWS) * slots, 2 * columns), bf16),
        pltpu.VMEM((WX, 2 * columns), jnp.float32),
        pltpu.VMEM((angle_devs, layers, share, 2 * columns), bf16),
        pltpu.VMEM((angle_devs, layers, share, 2 * columns), bf16),
        dma((REACHES, slots)),
        dma((REACHES, depths, half)),
        dma((depths,)),
        dma((depths,)),
        dma((REACHES, half, depths)),
        dma((REACHES, slots)),
        dma((angle_devs, layers)),
        dma((angle_devs, layers)),
    ]
    return pl.pallas_call(
        functools.partial(kernel, (strips, angle_devs, depths, layers, slots, columns)),
        out_shape=jax.ShapeDtypeStruct((layers, 2, share, columns), jnp.float32),
        in_specs=[vmem] * 5 + [smem] * 6,
        out_specs=vmem,
        scratch_shapes=scratch,
        compiler_params=pltpu.CompilerParams(collective_id=0, has_side_effects=True),
    )(
        crystal,
        probe,
        amplitude,
        table,
        table_t,
        shear,
        scan_x,
        scan_y,
        slot_angle,
        owner_slot,
        counts,
    )


def solution(mesh):
    placed = (
        P(("groups", "depth"), None, "strip", None),
        P(),
        P("angle", ("groups", "strip", "depth"), None),
        P(("groups", "angle"), "depth"),
        P(("groups", "angle"), None, None),
        P(("groups", "angle"), None, None),
        P(("groups", "angle"), None, None),
        P(("groups", "angle"), None, None),
        P(("groups", "angle"), None),
    )
    sizes_of = (mesh.shape["strip"], mesh.shape["angle"], mesh.shape["depth"])
    return jax.shard_map(
        functools.partial(body, sizes_of),
        mesh=mesh,
        in_specs=placed,
        out_specs=P(("groups", "depth"), None, ("strip", "angle"), None),
        check_vma=False,
    )
```

time: 374 us -> 38.1 us (0.10)
  local copies, waits for them, and re-layouts: 182 us -> 5.44 us
  loops' own time: 60.1 us -> 0 us
  waiting for transfers between devices: 46 us -> 0 us
  Pallas kernels: 0 us -> 32.4 us
  other arithmetic: 29.5 us -> 0 us
  blocking collectives: 21.1 us -> 0 us
  between operations: 13.6 us -> 0.01 us
  matrix products: 12.1 us -> 0 us
  starting transfers between devices: 7.15 us -> 0 us
    gather x122 -> x0, local copies, waits for them, and re-layouts: 78.9 us -> none
    dynamic_update_slice x24 -> x0, local copies, waits for them, and re-layouts: 71.4 us -> none  [deposit(): lax.dynamic_update_slice(gradient_pad, current + contribution[None], posi...]
    another operation x7 -> x0, loops' own time: 60.1 us -> none  [the longest x1 59.2 us: body(): gradient_pad = lax.fori_loop(0, 3 * slot_count, deposit, start_pad)]
    pallas_call x0 -> x1, Pallas kernels: none -> 32.4 us  [body(): pl.pallas_call(functools.partial(kernel, (strips, angle_devs, depths, lay...]
    all_to_all x1 -> x0, blocking collectives: 21.1 us -> none  [body(): lax.all_to_all(returning, 'strip', split_axis=0, concat_axis=0, tiled=True)]
    add x26 -> x0, other arithmetic: 20.3 us -> none  [the longest x24 20.2 us: deposit(): current + contribution[None]]
    reduce_scatter x1 -> x0, waiting for transfers between devices: 17.7 us -> none  [body(): lax.psum_scatter(gradient, 'angle', scatter_dimension=2, tiled=True)]
    unnamed x6 -> x0, waiting for transfers between devices: 15.2 us -> none
  transfers between devices with their start and end apart: 5 -> 0, of which waited for: 5 -> 0; matrix products, arithmetic and copies ran while one was open for 6% -> 0% of each run, Pallas kernels for 0% -> 0%
where the time goes in v1:
time: 38.1 us; the launch traced here: 37.9 us
  Pallas kernels  32.4 us (85%)
  local copies, waits for them, and re-layouts  5.44 us (14%)
    pallas_call x1, Pallas kernels, body(): pl.pallas_call(functools.partial(kernel, (strips, angle_devs, depths, lay...  32.4 us
    unnamed x11, local copies, waits for them, and re-layouts  5.44 us

profile of v1, /device:TPU:0, one launch (start us, length us, event | category | flops | bytes accessed | tf_op | source)
XLA Modules:
  0.0 37.9 jit_solution(16522895771889913772)
XLA Ops:
  0.0 0.0 copy-start
  0.0 1.3 %copy.12.scan_x = s32[1,4,2]{2,1,0:T(4,128)} copy(s32[1,4,2]{1,2,0:T(2,128)} %param.15) | data formatting | bytes 64 | tf_op args[4]
  1.4 0.0 copy-done
  1.4 0.0 copy-start.1
  1.4 0.7 %copy.13.scan_y = s32[1,4,2]{2,1,0:T(4,128)} copy(s32[1,4,2]{1,2,0:T(2,128)S(1)} %copy-done) | data formatting | bytes 64 | tf_op args[5]
  2.0 0.0 copy-done.1
  2.0 0.0 copy-start.2
  2.0 0.7 %copy.14.slot_angle = s32[1,4,2]{2,1,0:T(4,128)} copy(s32[1,4,2]{1,2,0:T(2,128)S(1)} %copy-done.1) | data formatting | bytes 64 | tf_op args[6]
  2.7 0.0 copy-done.2
  2.7 0.7 %copy.15.owner_slot = s32[1,4,2]{2,1,0:T(4,128)} copy(s32[1,4,2]{1,2,0:T(2,128)S(1)} %copy-done.2) | data formatting | bytes 64 | tf_op args[7]
  3.4 32.4 %shard_map.109 = f32[4,2,64,384]{3,2,1,0:T(8,128)} custom-call(bf16[4,2,128,384]{3,2,1,0:T(8,128)(2,1)} %crystal.1, bf16[2,256,256]{2,1,0:T(8,128)(2,1)} %probe.1, bf16[2,128,256]{2,1,0:T(8,128)(2,1)} %amplitude.1, bf16[512,512]{1,0:T(8,128)(2,1)} %constant.4.clone.table, bf16[512,512]{1,0:T(8,128)(2,1)} %constant.5.clone.table_t, s32[4,4]{1,0:T(4,128)} %shear.1, ...), custom_call_target="tpu_custom_call" | custom-call | tf_op jit(solution)/shard_map/pallas_call | solution.py:438
  35.8 2.1 %copy.17 = f32[4,2,64,384]{3,2,1,0:T(8,128)} copy(f32[4,2,64,384]{3,2,1,0:T(8,128)} %shard_map.109) | data formatting | bytes 1572864
Async XLA Ops:
  0.0 1.4 %copy-start = (s32[1,4,2]{1,2,0:T(2,128)S(1)}, s32[1,4,2]{1,2,0:T(2,128)}, u32[]{:S(2)}) copy-start(s32[1,4,2]{1,2,0:T(2,128)} %param.16) | copy-start | bytes 100
  1.4 0.7 %copy-start.1 = (s32[1,4,2]{1,2,0:T(2,128)S(1)}, s32[1,4,2]{1,2,0:T(2,128)}, u32[]{:S(2)}) copy-start(s32[1,4,2]{1,2,0:T(2,128)} %param.17) | copy-start | bytes 100
  2.0 0.7 %copy-start.2 = (s32[1,4,2]{1,2,0:T(2,128)S(1)}, s32[1,4,2]{1,2,0:T(2,128)}, u32[]{:S(2)}) copy-start(s32[1,4,2]{1,2,0:T(2,128)} %param.18) | copy-start | bytes 100

commit v2 on v1

v2 whole, which is shorter than its diff:
```python
import functools

import jax
import jax.numpy as jnp
import numpy as np
from jax import lax
from jax.experimental import pallas as pl
from jax.experimental.pallas import tpu as pltpu
from jax.sharding import PartitionSpec as P

FRAME = 256
WX = 128
SHEAR = 16
REACHES = 3
ROWS = (WX, FRAME, FRAME - WX)
BASES = (0, 0, WX)
MESH = pl.DeviceIdType.MESH


def dft_tables():
    index_row = np.arange(FRAME)
    phase = (index_row[:, None] * index_row[None, :] % FRAME) * (2.0 * np.pi / FRAME)
    real = np.cos(phase) / np.sqrt(FRAME)
    imag = -np.sin(phase) / np.sqrt(FRAME)
    table = np.block([[real, imag], [-imag, real]]).astype(np.float32)
    return jnp.asarray(table, jnp.bfloat16), jnp.asarray(table.T, jnp.bfloat16)


def dot(left, right):
    return jnp.dot(left, right, preferred_element_type=jnp.float32)


def differences(rows, columns):
    shape = (rows, columns)
    return lax.broadcasted_iota(jnp.int32, shape, 1) - lax.broadcasted_iota(jnp.int32, shape, 0)


def one_hot(mask):
    return jnp.where(mask, 1.0, 0.0).astype(jnp.bfloat16)


class Meta:
    def __init__(self, lifts, owner_slot, slots, lead):
        self.lifts, self.owner_slot = lifts, owner_slot
        self.slots, self.lead = slots, lead

    def shear(self, angle, z):
        return self.lifts[self.lead + (angle, z)]

    def pick(self, ref, home, quota):
        value = jnp.int32(0)
        for m in range(self.slots):
            at = self.lead + (0, m, home)
            value = value + jnp.where(self.owner_slot[at] == quota, ref[at], 0)
        return value

    def slot(self, home, quota):
        value = jnp.int32(0)
        for m in range(self.slots):
            at = self.lead + (0, m, home)
            value = value + jnp.where(self.owner_slot[at] == quota, m, 0)
        return value


def kernel(
    sizes,
    crystal,
    probe_in,
    amplitude,
    table_in,
    table_t_in,
    shear,
    scan_x,
    scan_y,
    slot_angle,
    owner_slot,
    counts,
    shear_in,
    scan_y_in,
    slot_angle_in,
    owner_slot_in,
    windows,
    shear_out,
    scan_y_out,
    slot_angle_out,
    owner_slot_out,
    film,
    probe,
    table,
    table_t,
    sent0,
    sent1,
    sent2,
    got0,
    got1,
    got2,
    measured,
    cuts,
    load_sem,
    film_send,
    film_recv,
    amp_send,
    amp_recv,
    meta_send,
    meta_recv,
    cut_send,
    pass_send,
    win_recv,
):
    strips, angle_devs, depths, layers, slots, columns = sizes
    quarter = strips // 4
    half = slots // depths
    share = WX // angle_devs
    reach = share + SHEAR
    sent = (sent0, sent1, sent2)
    got = (got0, got1, got2)
    s = lax.axis_index("strip")
    a = lax.axis_index("angle")
    d = lax.axis_index("depth")
    meta = Meta(shear, owner_slot, slots, ())

    def rcopy(source, target, send_sem, recv_sem, **where):
        return pltpu.make_async_remote_copy(
            source, target, send_sem, recv_sem, device_id=where, device_id_type=MESH
        )

    def wrap(strip):
        return lax.rem(strip + 4 * strips, strips)

    loads = [
        pltpu.make_async_copy(
            crystal.at[layer, part],
            film.at[layer * WX : (layer + 1) * WX, part * columns : (part + 1) * columns],
            load_sem.at[layer * 2 + part],
        )
        for layer in range(layers)
        for part in range(2)
    ]
    late = [
        pltpu.make_async_copy(source, target, load_sem.at[2 * layers + i])
        for i, (source, target) in enumerate(
            ((probe_in, probe), (table_in, table), (table_t_in, table_t))
        )
    ]
    for copy in loads + late:
        copy.start()

    barrier = pltpu.get_barrier_semaphore()
    shifts = set()
    for k in range(REACHES):
        for t in range(quarter):
            shifts |= {(1 - k + 4 * t) % strips, (k - 1 - 4 * t) % strips}
    expected = jnp.int32(0)
    for shift in sorted(shifts | {0}):
        peer = wrap(s + shift)
        if quarter == 1 and shift:
            close = jnp.abs(peer - s) == 1
        else:
            close = peer >= 0
        near = angle_devs + depths - 1 - (1 if shift == 0 else 0)
        expected = expected + jnp.where(close, near, 0)

        @pl.when(close)
        def _():
            for step in range(angle_devs):
                if shift or step:
                    place = {"strip": peer, "angle": lax.rem(a + step, angle_devs)}
                    pl.semaphore_signal(barrier, 1, device_id=place, device_id_type=MESH)
            for step in range(1, depths):
                place = {"strip": peer, "depth": lax.rem(d + step, depths)}
                pl.semaphore_signal(barrier, 1, device_id=place, device_id_type=MESH)

    for copy in loads:
        copy.wait()

    def film_copy(k, q):
        owner = wrap(s - k + 4 * (q % quarter) + 1)
        return rcopy(
            sent[k].at[q],
            got[k].at[d, q % half],
            film_send.at[k, q],
            film_recv.at[k, d, q % half],
            strip=owner,
            depth=q // half,
        )

    def own_strip(k, q):
        return (1 - k + 4 * (q % quarter)) % strips == 0

    def project(k, q):
        home = s - k
        offset = meta.pick(scan_x, home, q) - WX * k + BASES[k]
        angle = meta.pick(slot_angle, home, q)
        corner = meta.pick(scan_y, home, q)
        gap = differences(ROWS[k], WX)
        picks = jnp.concatenate(
            [one_hot(gap == offset + meta.shear(angle, z)) for z in range(layers)], axis=1
        )
        tall = dot(picks, film[...]).astype(jnp.bfloat16)
        window = one_hot(differences(columns, FRAME) == -corner)
        return jnp.concatenate(
            [dot(tall[:, :columns], window), dot(tall[:, columns:], window)], axis=1
        ).astype(jnp.bfloat16)

    def reached(k):
        return (s - k >= 0) & (s - k <= strips - 3)

    for k in (0, 2):

        @pl.when(reached(k))
        def _():
            for q in range(slots):
                sent[k][q] = project(k, q)

    pl.semaphore_wait(barrier, expected)

    for k in (0, 2):

        @pl.when(reached(k))
        def _():
            for q in range(slots):
                if own_strip(k, q):

                    @pl.when(d == q // half)
                    def _():
                        got[k][d, q % half] = sent[k][q]

                    @pl.when(d != q // half)
                    def _():
                        film_copy(k, q).start()
                else:
                    film_copy(k, q).start()

    def amp_copy(other):
        return rcopy(
            amplitude.at[other * half : (other + 1) * half],
            measured.at[d],
            amp_send.at[other],
            amp_recv.at[d],
            depth=other,
        )

    def amp_own(other):
        return pltpu.make_async_copy(
            amplitude.at[other * half : (other + 1) * half], measured.at[d], amp_recv.at[d]
        )

    tables = (
        (shear_in, shear_out),
        (scan_y_in, scan_y_out),
        (slot_angle_in, slot_angle_out),
        (owner_slot_in, owner_slot_out),
    )

    def meta_copies(step):
        return [
            rcopy(
                source,
                target.at[step],
                meta_send.at[step, i],
                meta_recv.at[step, i],
                angle=lax.rem(a + step, angle_devs),
            )
            for i, (source, target) in enumerate(tables)
        ]

    for other in range(depths):

        @pl.when(d != other)
        def _():
            amp_copy(other).start()

        @pl.when(d == other)
        def _():
            amp_own(other).start()

    for step in range(1, angle_devs):
        for copy in meta_copies(step):
            copy.start()

    @pl.when(reached(1))
    def _():
        for q in range(slots):
            if own_strip(1, q):

                @pl.when(d == q // half)
                def _():
                    got[1][d, q % half] = project(1, q)

                @pl.when(d != q // half)
                def _():
                    sent[1][q] = project(1, q)
                    film_copy(1, q).start()
            else:
                sent[1][q] = project(1, q)
                film_copy(1, q).start()

    for copy in late:
        copy.wait()
    for other in range(depths):

        @pl.when(d != other)
        def _():
            rcopy(
                amplitude.at[other * half : (other + 1) * half],
                measured.at[other],
                amp_send.at[other],
                amp_recv.at[other],
                depth=other,
            ).wait_recv()

        @pl.when(d == other)
        def _():
            amp_own(other).wait()

    for lane in range(half):
        quota = d * half + lane
        home = wrap(s - 1 - 4 * lax.rem(quota, quarter))

        @pl.when(home <= strips - 3)
        def _():
            for k in (1, 0, 2):
                for source in range(depths):
                    local = (wrap(home + k) == s) & (d == source)

                    @pl.when(jnp.logical_not(local))
                    def _():
                        rcopy(
                            sent[k].at[lane],
                            got[k].at[source, lane],
                            film_send.at[k, lane],
                            film_recv.at[k, source, lane],
                            strip=wrap(home + k),
                            depth=source,
                        ).wait_recv()

            def gathered(ref, low, high):
                value = ref[0, lane, low:high].astype(jnp.float32)
                for source in range(1, depths):
                    value = value + ref[source, lane, low:high].astype(jnp.float32)
                return value

            whole = jnp.concatenate(
                [
                    gathered(got1, 0, WX) + gathered(got0, 0, WX),
                    gathered(got1, WX, FRAME) + gathered(got2, 0, FRAME - WX),
                ],
                axis=0,
            )
            probe_re = probe[0].astype(jnp.float32)
            probe_im = probe[1].astype(jnp.float32)
            film_re, film_im = whole[:, :FRAME], whole[:, FRAME:]
            exit_wave = jnp.concatenate(
                [probe_re * film_re - probe_im * film_im, probe_re * film_im + probe_im * film_re],
                axis=1,
            ).astype(jnp.bfloat16)
            section = dot(exit_wave, table[...]).astype(jnp.bfloat16)
            spectrum = dot(
                table_t[...], jnp.concatenate([section[:, :FRAME], section[:, FRAME:]], axis=0)
            )
            spec_re, spec_im = spectrum[:FRAME], spectrum[FRAME:]
            magnitude = jnp.sqrt(spec_re * spec_re + spec_im * spec_im)
            levels = jnp.concatenate(
                [measured[source, lane] for source in range(depths)], axis=0
            ).astype(jnp.float32)
            live = meta.slot(home, quota) < counts[0, home]
            live = jnp.where(live, 1.0, 0.0).astype(jnp.float32)
            factor = (1.0 - levels / jnp.maximum(magnitude, 1.0)) * live
            residual = jnp.concatenate([spec_re * factor, spec_im * factor], axis=1).astype(
                jnp.bfloat16
            )
            inverse = dot(residual, table_t[...]).astype(jnp.bfloat16)
            wave = dot(
                table[...], jnp.concatenate([inverse[:, :FRAME], inverse[:, FRAME:]], axis=0)
            )
            wave_re, wave_im = wave[:FRAME], wave[FRAME:]
            back = jnp.concatenate(
                [probe_re * wave_re + probe_im * wave_im, probe_re * wave_im - probe_im * wave_re],
                axis=1,
            ).astype(jnp.bfloat16)
            offset = meta.pick(scan_x, home, quota)
            gap = differences(reach, FRAME)
            for k in (2, 0, 1):
                for part in range(angle_devs):
                    first = WX * k - offset + part * share - (SHEAR - 1)
                    cuts[lane, k, part] = dot(one_hot(gap == first), back).astype(jnp.bfloat16)

    def cut_copy(k, q, home, step):
        target = lax.rem(a + step, angle_devs)
        return rcopy(
            cuts.at[q % half, k, target],
            windows.at[step, k, q],
            cut_send.at[k, q % half, step],
            win_recv.at[step, k, q],
            strip=wrap(home + k),
            angle=target,
        )

    def cut_local(k, q):
        return pltpu.make_async_copy(
            cuts.at[q % half, k, a], windows.at[0, k, q], win_recv.at[0, k, q]
        )

    def pass_copy(step, k, q, other):
        return rcopy(
            windows.at[step, k, q],
            windows.at[step, k, q],
            pass_send.at[step, k, q % half, other],
            win_recv.at[step, k, q],
            depth=other,
        )

    def sends(act):
        for q in range(slots):
            home = wrap(s - 1 - 4 * (q % quarter))

            @pl.when((home <= strips - 3) & (d == q // half))
            def _():
                for step in list(range(1, angle_devs)) + [0]:
                    for k in (0, 2, 1):
                        if not (step == 0 and own_strip(k, q)):
                            act(cut_copy(k, q, home, step))

    sends(lambda copy: copy.start())

    for q in range(slots):
        home = wrap(s - 1 - 4 * (q % quarter))
        for k in range(REACHES):
            if own_strip(k, q):

                @pl.when((home <= strips - 3) & (d == q // half))
                def _():
                    cut_local(k, q).start()

    def relays(act):
        for step in range(angle_devs):
            for k in range(REACHES):

                @pl.when(reached(k))
                def _():
                    for q in range(slots):

                        @pl.when(d == q // half)
                        def _():
                            act(step, k, q)

    def relay(step, k, q):
        if step == 0 and own_strip(k, q):
            cut_local(k, q).wait()
        else:
            cut_copy(k, q, s - k, step).wait_recv()
        for other in range(depths):
            if other != q // half:
                pass_copy(step, k, q, other).start()

    relays(relay)

    for step in range(angle_devs):
        for k in range(REACHES):

            @pl.when(reached(k))
            def _():
                for q in range(slots):

                    @pl.when(d != q // half)
                    def _():
                        pass_copy(step, k, q, q // half).wait_recv()

    for step in range(1, angle_devs):
        for copy in meta_copies(step):
            copy.wait_recv()

    for other in range(depths):

        @pl.when(d != other)
        def _():
            amp_copy(other).wait_send()

    for step in range(1, angle_devs):
        for copy in meta_copies(step):
            copy.wait_send()
    for k in range(REACHES):

        @pl.when(reached(k))
        def _():
            for q in range(slots):
                if own_strip(k, q):

                    @pl.when(d != q // half)
                    def _():
                        film_copy(k, q).wait_send()
                else:
                    film_copy(k, q).wait_send()

    sends(lambda copy: copy.wait_send())

    def passed(step, k, q):
        for other in range(depths):
            if other != q // half:
                pass_copy(step, k, q, other).wait_send()

    relays(passed)


def deposit_kernel(
    sizes,
    scaling,
    windows,
    shear,
    scan_y,
    slot_angle,
    owner_slot,
    shears,
    scans_y,
    slot_angles,
    owner_slots,
    out,
    placed,
    total,
):
    strips, angle_devs, depths, layers, slots, columns = sizes
    share = WX // angle_devs
    reach = share + SHEAR
    s = lax.axis_index("strip")
    groups = [(Meta(shear, owner_slot, slots, ()), scan_y, slot_angle)]
    for step in range(1, angle_devs):
        groups.append((Meta(shears, owner_slots, slots, (step,)), scans_y, slot_angles))

    total[...] = jnp.zeros_like(total)
    for k in range(REACHES):
        home = s - k

        @pl.when((home >= 0) & (home <= strips - 3))
        def _():
            lifts = []
            for step in range(angle_devs):
                meta, corners, angles = groups[step]
                for q in range(slots):
                    at = (step * slots + q) * reach
                    window = one_hot(differences(FRAME, columns) == meta.pick(corners, home, q))
                    value = windows[step, k, q]
                    for part in range(2):
                        placed[at : at + reach, part * columns : (part + 1) * columns] = dot(
                            value[:, part * FRAME : (part + 1) * FRAME], window
                        ).astype(jnp.bfloat16)
                    angle = meta.pick(angles, home, q)
                    lifts.append([meta.shear(angle, z) for z in range(layers)])
            gap = differences(share, reach)
            for i, lift in enumerate(lifts):
                picks = jnp.concatenate(
                    [one_hot(gap == SHEAR - 1 - lift[z]) for z in range(layers)], axis=0
                )
                total[...] += dot(picks, placed[i * reach : (i + 1) * reach])

    for z in range(layers):
        for part in range(2):
            out[z, part] = (
                total[z * share : (z + 1) * share, part * columns : (part + 1) * columns] * scaling
            )


def body(sizes_of, crystal, probe, amplitude, shear, scan_x, scan_y, slot_angle, owner_slot, counts):
    strips, angle_devs, depths = sizes_of
    layers, _, _, columns = crystal.shape
    slots = owner_slot.shape[2]
    half = slots // depths
    share = WX // angle_devs
    reach = share + SHEAR
    table, table_t = dft_tables()
    bf16 = jnp.bfloat16
    scan_x, scan_y, slot_angle, owner_slot = [
        jnp.swapaxes(value, 1, 2) for value in (scan_x, scan_y, slot_angle, owner_slot)
    ]
    sizes = (strips, angle_devs, depths, layers, slots, columns)
    tables = (shear, scan_y, slot_angle, owner_slot)
    anywhere = pl.BlockSpec(memory_space=pl.ANY)
    vmem = pl.BlockSpec(memory_space=pltpu.VMEM)
    smem = pl.BlockSpec(memory_space=pltpu.SMEM)
    dma = pltpu.SemaphoreType.DMA
    scratch = [
        pltpu.VMEM((layers * WX, 2 * columns), bf16),
        pltpu.VMEM(probe.shape, bf16),
        pltpu.VMEM(table.shape, bf16),
        pltpu.VMEM(table.shape, bf16),
    ]
    scratch += [pltpu.VMEM((slots, rows, 2 * FRAME), bf16) for rows in ROWS]
    scratch += [pltpu.VMEM((depths, half, rows, 2 * FRAME), bf16) for rows in ROWS]
    scratch += [
        pltpu.VMEM((depths, half, FRAME // depths, FRAME), bf16),
        pltpu.VMEM((half, REACHES, angle_devs, reach, 2 * FRAME), bf16),
        dma((2 * layers + 3,)),
        dma((REACHES, slots)),
        dma((REACHES, depths, half)),
        dma((depths,)),
        dma((depths,)),
        dma((angle_devs, len(tables))),
        dma((angle_devs, len(tables))),
        dma((REACHES, half, angle_devs)),
        dma((angle_devs, REACHES, half, depths)),
        dma((angle_devs, REACHES, slots)),
    ]
    windows, *others = pl.pallas_call(
        functools.partial(kernel, sizes),
        out_shape=(
            jax.ShapeDtypeStruct((angle_devs, REACHES, slots, reach, 2 * FRAME), bf16),
        )
        + tuple(jax.ShapeDtypeStruct((angle_devs,) + x.shape, jnp.int32) for x in tables),
        in_specs=[anywhere] * 5 + [smem] * 6 + [anywhere] * 4,
        out_specs=(anywhere,) * 5,
        scratch_shapes=scratch,
        compiler_params=pltpu.CompilerParams(collective_id=0, has_side_effects=True),
    )(
        crystal,
        probe,
        amplitude,
        table,
        table_t,
        shear,
        scan_x,
        scan_y,
        slot_angle,
        owner_slot,
        counts,
        *tables,
    )
    scaling = 1.0 / (shear.shape[0] * angle_devs)
    return pl.pallas_call(
        functools.partial(deposit_kernel, sizes, scaling),
        out_shape=jax.ShapeDtypeStruct((layers, 2, share, columns), jnp.float32),
        in_specs=[vmem] + [smem] * 8,
        out_specs=vmem,
        scratch_shapes=[
            pltpu.VMEM((angle_devs * slots * reach, 2 * columns), bf16),
            pltpu.VMEM((layers * share, 2 * columns), jnp.float32),
        ],
    )(windows, *tables, *others)


def solution(mesh):
    placed = (
        P(("groups", "depth"), None, "strip", None),
        P(),
        P("angle", ("groups", "strip", "depth"), None),
        P(("groups", "angle"), "depth"),
        P(("groups", "angle"), None, None),
        P(("groups", "angle"), None, None),
        P(("groups", "angle"), None, None),
        P(("groups", "angle"), None, None),
        P(("groups", "angle"), None),
    )
    sizes_of = (mesh.shape["strip"], mesh.shape["angle"], mesh.shape["depth"])
    return jax.shard_map(
        functools.partial(body, sizes_of),
        mesh=mesh,
        in_specs=placed,
        out_specs=P(("groups", "depth"), None, ("strip", "angle"), None),
        check_vma=False,
    )
```

time: 38.1 us -> 24.4 us (0.64)
  Pallas kernels: 32.4 us -> 24.2 us
  local copies, waits for them, and re-layouts: 5.44 us -> 0 us
    pallas_call x1 -> x2, Pallas kernels: 32.4 us -> 24.2 us  [the longest x1 21.1 us: body(): pl.pallas_call(functools.partial(kernel, sizes), out_shape=(jax.ShapeDtyp...]
    unnamed x11 -> x0, local copies, waits for them, and re-layouts: 5.44 us -> none
where the time goes in v2:
time: 24.4 us; the launch traced here: 24.2 us
  Pallas kernels  24.2 us (99%)
    pallas_call x1, Pallas kernels, body(): pl.pallas_call(functools.partial(kernel, sizes), out_shape=(jax.ShapeDtyp...  21.1 us
    pallas_call x1, Pallas kernels, body(): pl.pallas_call(functools.partial(deposit_kernel, sizes, scaling), out_sha...  3.03 us

profile of v2, /device:TPU:0, one launch (start us, length us, event | category | flops | bytes accessed | tf_op | source)
XLA Modules:
  0.0 24.2 jit_solution(17886405844402968102)
XLA Ops:
  0.0 21.1 %shard_map.109 = (bf16[2,3,2,80,512]{4,3,2,1,0:T(8,128)(2,1)}, s32[2,4,4]{2,1,0:T(4,128)}, s32[2,1,2,4]{3,2,1,0:T(2,128)}, s32[2,1,2,4]{3,2,1,0:T(2,128)}, s32[2,1,2,4]{3,2,1,0:T(2,128)}) custom-call(bf16[4,2,128,384]{3,2,1,0:T(8,128)(2,1)} %crystal.1, bf16[2,256,256]{2,1,0:T(8,128)(2,1)} %probe_in.1, bf16[2,128,256]{2,1,0:T(8,128)(2,1)} %amplitude.1, ...), custom_call_target="tpu_custom_call" | custom-call | tf_op jit(solution)/shard_map/pallas_call | solution.py:602
  21.1 3.0 %shard_map.110 = f32[4,2,64,384]{3,2,1,0:T(8,128)} custom-call(bf16[2,3,2,80,512]{4,3,2,1,0:T(8,128)(2,1)} %get-tuple-element.10.windows, s32[4,4]{1,0:T(4,128)} %shear.3, s32[1,2,4]{2,1,0:T(2,128)} %bitcast.6, s32[1,2,4]{2,1,0:T(2,128)} %bitcast.9, s32[1,2,4]{2,1,0:T(2,128)} %bitcast.12, s32[2,4,4]{2,1,0:T(4,128)} %get-tuple-element.11.shears, ...), custom_call_target="tpu_custom_call" | custom-call | tf_op jit(solution)/shard_map/pallas_call | solution.py:627

commit v3 on v2

--- a/solution.py
+++ b/solution.py
@@ -94,11 +94,22 @@
     got0,
     got1,
     got2,
+    mix0,
+    mix1,
+    mix2,
+    part0,
+    part1,
+    part2,
+    own,
     measured,
     cuts,
     load_sem,
     film_send,
     film_recv,
+    mix_send,
+    mix_recv,
+    own_send,
+    own_recv,
     amp_send,
     amp_recv,
     meta_send,
@@ -114,6 +125,8 @@
     reach = share + SHEAR
     sent = (sent0, sent1, sent2)
     got = (got0, got1, got2)
+    mix = (mix0, mix1, mix2)
+    parts = (part0, part1, part2)
     s = lax.axis_index("strip")
     a = lax.axis_index("angle")
     d = lax.axis_index("depth")
@@ -173,16 +186,50 @@
     for copy in loads:
         copy.wait()
 
+    def block(k, device):
+        rows = ROWS[k] // depths
+        return pl.ds(pl.multiple_of(device * rows, rows), rows)
+
+    def mix_copy(k, q, step):
+        target = lax.rem(d + step, depths)
+        return rcopy(
+            sent[k].at[q, block(k, target)],
+            mix[k].at[q, step],
+            mix_send.at[k, q, step],
+            mix_recv.at[k, q, step],
+            depth=target,
+        )
+
     def film_copy(k, q):
-        owner = wrap(s - k + 4 * (q % quarter) + 1)
         return rcopy(
-            sent[k].at[q],
-            got[k].at[d, q % half],
+            parts[k].at[q],
+            got[k].at[q % half, block(k, d)],
             film_send.at[k, q],
             film_recv.at[k, d, q % half],
-            strip=owner,
+            strip=wrap(s - k + 4 * (q % quarter) + 1),
             depth=q // half,
         )
+
+    def own_copy(q):
+        return rcopy(
+            sent[1].at[q],
+            own.at[d, q % half],
+            own_send.at[q],
+            own_recv.at[d, q % half],
+            depth=q // half,
+        )
+
+    def exchange(k, q):
+        for step in range(1, depths):
+            mix_copy(k, q, step).start()
+
+    def merge(k, q):
+        value = sent[k][q, block(k, d)].astype(jnp.float32)
+        for step in range(1, depths):
+            mix_copy(k, q, step).wait_recv()
+            value = value + mix[k][q, step].astype(jnp.float32)
+        parts[k][q] = value.astype(jnp.bfloat16)
+        film_copy(k, q).start()
 
     def own_strip(k, q):
         return (1 - k + 4 * (q % quarter)) % strips == 0
@@ -205,31 +252,27 @@
     def reached(k):
         return (s - k >= 0) & (s - k <= strips - 3)
 
-    for k in (0, 2):
-
-        @pl.when(reached(k))
-        def _():
-            for q in range(slots):
+    for q in range(slots):
+        for k in (0, 2):
+
+            @pl.when(reached(k))
+            def _():
                 sent[k][q] = project(k, q)
 
-    pl.semaphore_wait(barrier, expected)
-
-    for k in (0, 2):
-
-        @pl.when(reached(k))
-        def _():
-            for q in range(slots):
-                if own_strip(k, q):
-
-                    @pl.when(d == q // half)
-                    def _():
-                        got[k][d, q % half] = sent[k][q]
-
-                    @pl.when(d != q // half)
-                    def _():
-                        film_copy(k, q).start()
-                else:
-                    film_copy(k, q).start()
+        if q == 0:
+            pl.semaphore_wait(barrier, expected)
+        for k in (0, 2):
+
+            @pl.when(reached(k))
+            def _():
+                exchange(k, q)
+
+    for q in range(slots):
+        for k in (0, 2):
+
+            @pl.when(reached(k))
+            def _():
+                merge(k, q)
 
     def amp_copy(other):
         return rcopy(
@@ -281,19 +324,21 @@
     @pl.when(reached(1))
     def _():
         for q in range(slots):
+            sent[1][q] = project(1, q)
             if own_strip(1, q):
 
                 @pl.when(d == q // half)
                 def _():
-                    got[1][d, q % half] = project(1, q)
+                    own[d, q % half] = sent[1][q]
 
                 @pl.when(d != q // half)
                 def _():
-                    sent[1][q] = project(1, q)
-                    film_copy(1, q).start()
+                    own_copy(q).start()
             else:
-                sent[1][q] = project(1, q)
-                film_copy(1, q).start()
+                exchange(1, q)
+        for q in range(slots):
+            if not own_strip(1, q):
+                merge(1, q)
 
     for copy in late:
         copy.wait()
@@ -319,26 +364,44 @@
 
         @pl.when(home <= strips - 3)
         def _():
-            for k in (1, 0, 2):
+            def arrive(k):
                 for source in range(depths):
-                    local = (wrap(home + k) == s) & (d == source)
-
-                    @pl.when(jnp.logical_not(local))
-                    def _():
-                        rcopy(
-                            sent[k].at[lane],
-                            got[k].at[source, lane],
-                            film_send.at[k, lane],
-                            film_recv.at[k, source, lane],
-                            strip=wrap(home + k),
-                            depth=source,
-                        ).wait_recv()
+                    rows = ROWS[k] // depths
+                    rcopy(
+                        parts[k].at[lane],
+                        got[k].at[lane, source * rows : (source + 1) * rows],
+                        film_send.at[k, lane],
+                        film_recv.at[k, source, lane],
+                        strip=wrap(home + k),
+                        depth=source,
+                    ).wait_recv()
+
+            local = wrap(home + 1) == s
+
+            @pl.when(local)
+            def _():
+                value = own[d, lane].astype(jnp.float32)
+                for step in range(1, depths):
+                    source = lax.rem(d + step, depths)
+                    rcopy(
+                        sent[1].at[lane],
+                        own.at[source, lane],
+                        own_send.at[lane],
+                        own_recv.at[source, lane],
+                        depth=source,
+                    ).wait_recv()
+                    value = value + own[source, lane].astype(jnp.float32)
+                got[1][lane] = value.astype(jnp.bfloat16)
+
+            @pl.when(jnp.logical_not(local))
+            def _():
+                arrive(1)
+
+            arrive(0)
+            arrive(2)
 
             def gathered(ref, low, high):
-                value = ref[0, lane, low:high].astype(jnp.float32)
-                for source in range(1, depths):
-                    value = value + ref[source, lane, low:high].astype(jnp.float32)
-                return value
+                return ref[lane, low:high].astype(jnp.float32)
 
             whole = jnp.concatenate(
                 [
@@ -488,9 +551,11 @@
 
                     @pl.when(d != q // half)
                     def _():
-                        film_copy(k, q).wait_send()
+                        own_copy(q).wait_send()
                 else:
                     film_copy(k, q).wait_send()
+                    for step in range(1, depths):
+                        mix_copy(k, q, step).wait_send()
 
     sends(lambda copy: copy.wait_send())
 
@@ -584,13 +649,20 @@
         pltpu.VMEM(table.shape, bf16),
     ]
     scratch += [pltpu.VMEM((slots, rows, 2 * FRAME), bf16) for rows in ROWS]
-    scratch += [pltpu.VMEM((depths, half, rows, 2 * FRAME), bf16) for rows in ROWS]
+    scratch += [pltpu.VMEM((half, rows, 2 * FRAME), bf16) for rows in ROWS]
+    scratch += [pltpu.VMEM((slots, depths, rows // depths, 2 * FRAME), bf16) for rows in ROWS]
+    scratch += [pltpu.VMEM((slots, rows // depths, 2 * FRAME), bf16) for rows in ROWS]
+    scratch += [pltpu.VMEM((depths, half, FRAME, 2 * FRAME), bf16)]
     scratch += [
         pltpu.VMEM((depths, half, FRAME // depths, FRAME), bf16),
         pltpu.VMEM((half, REACHES, angle_devs, reach, 2 * FRAME), bf16),
         dma((2 * layers + 3,)),
         dma((REACHES, slots)),
         dma((REACHES, depths, half)),
+        dma((REACHES, slots, depths)),
+        dma((REACHES, slots, depths)),
+        dma((slots,)),
+        dma((depths, half)),
         dma((depths,)),
         dma((depths,)),
         dma((angle_devs, len(tables))),

time: 24.4 us -> 23.8 us (0.975)
  Pallas kernels: 24.2 us -> 23.5 us
    pallas_call x1, Pallas kernels: 21.1 us -> 20.5 us  [body(): pl.pallas_call(functools.partial(kernel, sizes), out_shape=(jax.ShapeDtyp...]
where the time goes in v3:
time: 23.8 us; the launch traced here: 23.5 us
  Pallas kernels  23.5 us (99%)
    pallas_call x1, Pallas kernels, body(): pl.pallas_call(functools.partial(kernel, sizes), out_shape=(jax.ShapeDtyp...  20.5 us
    pallas_call x1, Pallas kernels, body(): pl.pallas_call(functools.partial(deposit_kernel, sizes, scaling), out_sha...  3.03 us

profile of v3, /device:TPU:0, one launch (start us, length us, event | category | flops | bytes accessed | tf_op | source)
XLA Modules:
  0.0 23.5 jit_solution(7584466127671976822)
XLA Ops:
  0.0 20.5 %shard_map.109 = (bf16[2,3,2,80,512]{4,3,2,1,0:T(8,128)(2,1)}, s32[2,4,4]{2,1,0:T(4,128)}, s32[2,1,2,4]{3,2,1,0:T(2,128)}, s32[2,1,2,4]{3,2,1,0:T(2,128)}, s32[2,1,2,4]{3,2,1,0:T(2,128)}) custom-call(bf16[4,2,128,384]{3,2,1,0:T(8,128)(2,1)} %crystal.1, bf16[2,256,256]{2,1,0:T(8,128)(2,1)} %probe_in.1, bf16[2,128,256]{2,1,0:T(8,128)(2,1)} %amplitude.1, ...), custom_call_target="tpu_custom_call" | custom-call | tf_op jit(solution)/shard_map/pallas_call | solution.py:674
  20.5 3.0 %shard_map.110 = f32[4,2,64,384]{3,2,1,0:T(8,128)} custom-call(bf16[2,3,2,80,512]{4,3,2,1,0:T(8,128)(2,1)} %get-tuple-element.10.windows, s32[4,4]{1,0:T(4,128)} %shear.3, s32[1,2,4]{2,1,0:T(2,128)} %bitcast.6, s32[1,2,4]{2,1,0:T(2,128)} %bitcast.9, s32[1,2,4]{2,1,0:T(2,128)} %bitcast.12, s32[2,4,4]{2,1,0:T(4,128)} %get-tuple-element.11.shears, ...), custom_call_target="tpu_custom_call" | custom-call | tf_op jit(solution)/shard_map/pallas_call | solution.py:699

commit v4 on v3

--- a/solution.py
+++ b/solution.py
@@ -586,12 +586,17 @@
     strips, angle_devs, depths, layers, slots, columns = sizes
     share = WX // angle_devs
     reach = share + SHEAR
+    stride = -(-reach // 128) * 128
     s = lax.axis_index("strip")
+    first = jnp.maximum(s - strips + 3, 0)
     groups = [(Meta(shear, owner_slot, slots, ()), scan_y, slot_angle)]
     for step in range(1, angle_devs):
         groups.append((Meta(shears, owner_slots, slots, (step,)), scans_y, slot_angles))
 
-    total[...] = jnp.zeros_like(total)
+    for i in range(angle_devs * slots):
+        placed[i * stride + reach : (i + 1) * stride] = jnp.zeros(
+            (stride - reach, 2 * columns), jnp.bfloat16
+        )
     for k in range(REACHES):
         home = s - k
 
@@ -601,21 +606,35 @@
             for step in range(angle_devs):
                 meta, corners, angles = groups[step]
                 for q in range(slots):
-                    at = (step * slots + q) * reach
-                    window = one_hot(differences(FRAME, columns) == meta.pick(corners, home, q))
-                    value = windows[step, k, q]
+                    at = (step * slots + q) * stride
+                    corner = meta.pick(corners, home, q)
+                    value = windows[step, k, q].astype(jnp.float32)
+                    margin = jnp.zeros((reach, columns - FRAME), jnp.float32)
                     for part in range(2):
-                        placed[at : at + reach, part * columns : (part + 1) * columns] = dot(
-                            value[:, part * FRAME : (part + 1) * FRAME], window
+                        wide = jnp.concatenate(
+                            [value[:, part * FRAME : (part + 1) * FRAME], margin], axis=1
+                        )
+                        placed[at : at + reach, part * columns : (part + 1) * columns] = pltpu.roll(
+                            wide, corner, 1
                         ).astype(jnp.bfloat16)
                     angle = meta.pick(angles, home, q)
                     lifts.append([meta.shear(angle, z) for z in range(layers)])
-            gap = differences(share, reach)
-            for i, lift in enumerate(lifts):
-                picks = jnp.concatenate(
-                    [one_hot(gap == SHEAR - 1 - lift[z]) for z in range(layers)], axis=0
-                )
-                total[...] += dot(picks, placed[i * reach : (i + 1) * reach])
+            gap = differences(share, stride)
+            picks = jnp.concatenate(
+                [
+                    jnp.concatenate([one_hot(gap == SHEAR - 1 - lift[z]) for lift in lifts], axis=1)
+                    for z in range(layers)
+                ],
+                axis=0,
+            )
+
+            @pl.when(first == k)
+            def _():
+                total[...] = dot(picks, placed[...])
+
+            @pl.when(first != k)
+            def _():
+                total[...] += dot(picks, placed[...])
 
     for z in range(layers):
         for part in range(2):
@@ -631,6 +650,7 @@
     half = slots // depths
     share = WX // angle_devs
     reach = share + SHEAR
+    stride = -(-reach // 128) * 128
     table, table_t = dft_tables()
     bf16 = jnp.bfloat16
     scan_x, scan_y, slot_angle, owner_slot = [
@@ -702,7 +722,7 @@
         in_specs=[vmem] + [smem] * 8,
         out_specs=vmem,
         scratch_shapes=[
-            pltpu.VMEM((angle_devs * slots * reach, 2 * columns), bf16),
+            pltpu.VMEM((angle_devs * slots * stride, 2 * columns), bf16),
             pltpu.VMEM((layers * share, 2 * columns), jnp.float32),
         ],
     )(windows, *tables, *others)

time: 23.8 us -> 23.5 us (0.987)
  no operation moved by 1% of the time
where the time goes in v4:
time: 23.5 us; the launch traced here: 23.3 us
  Pallas kernels  23.3 us (99%)
    pallas_call x1, Pallas kernels, body(): pl.pallas_call(functools.partial(kernel, sizes), out_shape=(jax.ShapeDtyp...  20.5 us
    pallas_call x1, Pallas kernels, body(): pl.pallas_call(functools.partial(deposit_kernel, sizes, scaling), out_sha...  2.79 us

profile of v4, /device:TPU:0, one launch (start us, length us, event | category | flops | bytes accessed | tf_op | source)
XLA Modules:
  0.0 23.3 jit_solution(9596852965407301351)
XLA Ops:
  0.0 20.5 %shard_map.109 = (bf16[2,3,2,80,512]{4,3,2,1,0:T(8,128)(2,1)}, s32[2,4,4]{2,1,0:T(4,128)}, s32[2,1,2,4]{3,2,1,0:T(2,128)}, s32[2,1,2,4]{3,2,1,0:T(2,128)}, s32[2,1,2,4]{3,2,1,0:T(2,128)}) custom-call(bf16[4,2,128,384]{3,2,1,0:T(8,128)(2,1)} %crystal.1, bf16[2,256,256]{2,1,0:T(8,128)(2,1)} %probe_in.1, bf16[2,128,256]{2,1,0:T(8,128)(2,1)} %amplitude.1, ...), custom_call_target="tpu_custom_call" | custom-call | tf_op jit(solution)/shard_map/pallas_call | solution.py:694
  20.5 2.8 %shard_map.110 = f32[4,2,64,384]{3,2,1,0:T(8,128)} custom-call(bf16[2,3,2,80,512]{4,3,2,1,0:T(8,128)(2,1)} %get-tuple-element.10.windows, s32[4,4]{1,0:T(4,128)} %shear.3, s32[1,2,4]{2,1,0:T(2,128)} %bitcast.6, s32[1,2,4]{2,1,0:T(2,128)} %bitcast.9, s32[1,2,4]{2,1,0:T(2,128)} %bitcast.12, s32[2,4,4]{2,1,0:T(4,128)} %get-tuple-element.11.shears, ...), custom_call_target="tpu_custom_call" | custom-call | tf_op jit(solution)/shard_map/pallas_call | solution.py:719
